TPU v7x, 32 devices: a whole 2x2x4 slice. The times are simulated.
32 devices in a mesh: ha: 4 (over y, x), wa: 8 (over z, core).
Axes of the slice: x: 2, y: 2, z: 4, core: 2. Of those that a mesh axis runs over, the one named last changes fastest.
Arguments:
- inputs: bfloat16 [32, 8, 16, 1536], P(None, 'ha', 'wa'), may hold values from -6 to 6
- query_vectors: bfloat16 [32, 8, 16, 1536], P(None, 'ha', 'wa'), may hold values from -256 to 256
- key_vectors: bfloat16 [32, 8, 16, 1536], P(None, 'ha', 'wa'), may hold values from -32 to 32
- value_vectors: bfloat16 [32, 8, 16, 1536], P(None, 'ha', 'wa'), may hold values from -6 to 6
- output_cotangent: bfloat16 [32, 8, 16, 1536], P(None, 'ha', 'wa'), may hold values from -6 to 6
- window: int32 [12, 4], replicated, may hold values from 0 to 2, as said below
Outputs:
- attention_output: bfloat16 [32, 8, 16, 1536], P(None, 'ha', 'wa')
- key_gradient: bfloat16 [32, 8, 16, 1536], P(None, 'ha', 'wa')
- value_gradient: bfloat16 [32, 8, 16, 1536], P(None, 'ha', 'wa')
- weight_gradient: bfloat16 [1536, 1536], P('wa', 'ha')
Inputs may be any that keep to these rules, and one draw needn't show every extreme that they name: `window`: row n is head n's (tile size s, reach in tiles along frames, reach in cells along rows, reach in cells along columns) with s one of 1, 2, the frame reach 0 to 2 and s times the frame reach at most 2, the row and column reaches 0 or 1; some head has s = 2 and reaches 1, 1, 1.
All inputs are finite; a program needn't handle non-finite values.
Results may differ from a plain program's by a relative error of at most 0.035.
Values may be sent and summed in bfloat16 or wider, within the bound.
A program may use at most 128 MiB of HBM per device.

v0:
```python
import functools
import math

import jax
import jax.numpy as jnp
from jax import lax
from jax.experimental import pallas as pl
from jax.experimental.pallas import tpu as pltpu
from jax.sharding import PartitionSpec as P

MESH = pl.DeviceIdType.MESH
GROUPS = 4


def attention_kernel(
    groups,
    window_hbm,
    q_ref,
    do_ref,
    own_ref,
    x_ref,
    att_ref,
    grad_ref,
    weight_ref,
    window_ref,
    padded,
    terms,
    from_side,
    from_row,
    slopes_own,
    x_all,
    slopes_all,
    product,
    from_partner,
    pair_sums,
    from_chips,
    local_sem,
    send_sem,
    recv_sem,
    x_send,
    x_recv,
    forward_send,
    forward_recv,
    slope_send,
    slope_recv,
    pair_send,
    pair_recv,
    chip_send,
    chip_recv,
):
    head_count, _, rows, columns, frames, head_size = own_ref.shape
    per_group = head_count // groups
    scale = 1.0 / math.sqrt(head_size)
    ha_count, wa_count = lax.axis_size("ha"), lax.axis_size("wa")
    ha, wa = lax.axis_index("ha"), lax.axis_index("wa")
    exists = {
        ("ha", -1): ha > 0,
        ("ha", 1): ha < ha_count - 1,
        ("wa", -1): wa > 0,
        ("wa", 1): wa < wa_count - 1,
    }
    place = {"ha": ha, "wa": wa}

    center = pltpu.make_async_copy(
        own_ref, padded.at[:, :, pl.ds(1, rows), pl.ds(1, columns)], local_sem.at[0]
    )
    center.start()
    unit = slopes_own.shape[2]
    share = slopes_all.shape[1]
    core, chip = wa % 2, wa // 2
    chips = wa_count // 2
    own_x = pltpu.make_async_copy(x_ref, x_all.at[ha], local_sem.at[1])
    own_x.start()
    window_copy = pltpu.make_async_copy(window_hbm, window_ref, local_sem.at[2])
    window_copy.start()

    @pl.when(ha == 0)
    def _():
        padded[:, :, 0] = jnp.zeros(padded.shape[:2] + padded.shape[3:], padded.dtype)
        from_row[0] = jnp.zeros(from_row.shape[1:], from_row.dtype)

    @pl.when(ha == ha_count - 1)
    def _():
        padded[:, :, rows + 1] = jnp.zeros(padded.shape[:2] + padded.shape[3:], padded.dtype)
        from_row[1] = jnp.zeros(from_row.shape[1:], from_row.dtype)

    @pl.when(wa == 0)
    def _():
        padded[:, :, :, 0] = jnp.zeros(padded.shape[:3] + padded.shape[4:], padded.dtype)
        from_side[0] = jnp.zeros(from_side.shape[1:], from_side.dtype)

    @pl.when(wa == wa_count - 1)
    def _():
        padded[:, :, :, columns + 1] = jnp.zeros(
            padded.shape[:3] + padded.shape[4:], padded.dtype
        )
        from_side[1] = jnp.zeros(from_side.shape[1:], from_side.dtype)

    barrier = pltpu.get_barrier_semaphore()
    for axis, count in (("ha", ha_count), ("wa", wa_count)):
        for step in range(1, count):
            pl.semaphore_signal(
                barrier,
                inc=1,
                device_id={axis: (place[axis] + step) % count},
                device_id_type=MESH,
            )
    pl.semaphore_wait(barrier, ha_count + wa_count - 2)

    def copy_of(phase, by, group):
        heads = pl.ds(group * per_group, per_group)
        inner_columns = pl.ds(1, columns)
        low = by < 0
        if phase == 0:
            source = own_ref.at[heads, :, 0 if low else rows - 1]
            target = padded.at[heads, :, rows + 1 if low else 0, inner_columns]
        elif phase == 1:
            source = padded.at[heads, :, :, 1 if low else columns]
            target = padded.at[heads, :, :, columns + 1 if low else 0]
        elif phase == 2:
            source = terms.at[heads, :, :, 0 if low else columns + 1]
            target = from_side.at[1 if low else 0, heads]
        else:
            source = terms.at[heads, :, 0 if low else rows + 1, inner_columns]
            target = from_row.at[1 if low else 0, heads]
        axis = "ha" if phase in (0, 3) else "wa"
        side = 0 if low else 1
        return axis, pltpu.make_async_remote_copy(
            src_ref=source,
            dst_ref=target,
            send_sem=send_sem.at[phase, side, group],
            recv_sem=recv_sem.at[phase, side, group],
            device_id={axis: place[axis] + by},
            device_id_type=MESH,
        )

    def start(phase, group):
        for by in (-1, 1):
            axis, copy = copy_of(phase, by, group)

            @pl.when(exists[axis, by])
            def _():
                copy.start()

    def arrived(phase, group):
        for by in (-1, 1):
            axis, copy = copy_of(phase, by, group)

            @pl.when(exists[axis, -by])
            def _():
                copy.wait_recv()

    def sent(phase, group):
        for by in (-1, 1):
            axis, copy = copy_of(phase, by, group)

            @pl.when(exists[axis, by])
            def _():
                copy.wait_send()

    def x_copy(peer):
        return pltpu.make_async_remote_copy(
            src_ref=x_ref,
            dst_ref=x_all.at[ha],
            send_sem=x_send.at[peer],
            recv_sem=x_recv.at[ha],
            device_id={"ha": peer},
            device_id_type=MESH,
        )

    low, high = ha % 2, ha // 2
    partner = 2 * high + 1 - low
    pairs = ha_count // 2
    half = x_ref.shape[0] // 2

    def forward_copy(part, slot, peer, mark):
        tokens = pl.ds(part * half, half)
        return pltpu.make_async_remote_copy(
            src_ref=x_all.at[slot, tokens],
            dst_ref=x_all.at[slot, tokens],
            send_sem=forward_send.at[part, mark],
            recv_sem=forward_recv.at[part, slot],
            device_id={"ha": peer},
            device_id_type=MESH,
        )

    def slope_copy(peer):
        return pltpu.make_async_remote_copy(
            src_ref=slopes_own.at[pl.ds(peer * share, share)],
            dst_ref=slopes_all.at[ha],
            send_sem=slope_send.at[peer],
            recv_sem=slope_recv.at[ha],
            device_id={"ha": peer},
            device_id_type=MESH,
        )

    def chip_copy(peer):
        return pltpu.make_async_remote_copy(
            src_ref=pair_sums.at[peer],
            dst_ref=from_chips.at[chip],
            send_sem=chip_send.at[peer],
            recv_sem=chip_recv.at[chip],
            device_id={"wa": 2 * peer + core},
            device_id_type=MESH,
        )

    def pair_copy(step):
        return pltpu.make_async_remote_copy(
            src_ref=product.at[step, 1 - core],
            dst_ref=from_partner.at[step],
            send_sem=pair_send.at[step],
            recv_sem=pair_recv.at[step],
            device_id={"wa": wa + 1 - 2 * core},
            device_id_type=MESH,
        )

    def landed(buffer, sems, peer):
        pltpu.make_async_copy(buffer.at[peer], buffer.at[peer], sems.at[peer]).wait()

    for group in range(groups):
        start(0, group)
    x_copy(partner).start()
    for pair in range(pairs):

        @pl.when(pair != high)
        def _(pair=pair):
            x_copy(2 * pair + low).start()

    center.wait()
    window_copy.wait()

    queries = rows * columns * frames
    keys = (rows + 2) * (columns + 2) * frames
    query_id = lax.broadcasted_iota(jnp.int32, (queries, 1), 0)
    key_id = lax.broadcasted_iota(jnp.int32, (1, keys), 1)
    query_frame = query_id % frames
    query_row = query_id // (frames * columns)
    query_column = (query_id // frames) % columns
    key_frame = key_id % frames
    key_row = key_id // (frames * (columns + 2)) - 1
    key_column = (key_id // frames) % (columns + 2) - 1
    outside = (
        (key_row + ha * rows < 0)
        | (key_row + ha * rows >= ha_count * rows)
        | (key_column + wa * columns < 0)
        | (key_column + wa * columns >= wa_count * columns)
    )
    key_row = jnp.where(outside, 1000, key_row)
    row_gap = jnp.abs(query_row - key_row)
    column_gap = jnp.abs(query_column - key_column)

    def head_step(head, carry):
        tile = window_ref[head, 0]
        q = q_ref[head].reshape(queries, head_size)
        do = do_ref[head].reshape(queries, head_size)
        k = padded[head, 0].reshape(keys, head_size)
        v = padded[head, 1].reshape(keys, head_size)
        query_tile = jnp.where(tile == 2, query_frame >> 1, query_frame)
        key_tile = jnp.where(tile == 2, key_frame >> 1, key_frame)
        allowed = (
            (jnp.abs(query_tile - key_tile) <= window_ref[head, 1])
            & (row_gap <= window_ref[head, 2])
            & (column_gap <= window_ref[head, 3])
        )
        across = (((1,), (1,)), ((), ()))
        down = (((0,), (0,)), ((), ()))
        dot = functools.partial(lax.dot_general, preferred_element_type=jnp.float32)
        scores = jnp.where(allowed, dot(q, k, across) * scale, -jnp.inf)
        top = jnp.max(scores, axis=1, keepdims=True)
        lifted = jnp.exp(scores - top)
        total = jnp.sum(lifted, axis=1, keepdims=True)
        weight = (lifted * (1.0 / total)).astype(jnp.bfloat16)
        att = jnp.dot(weight, v, preferred_element_type=jnp.float32).astype(jnp.bfloat16)
        att_ref[head] = att.reshape(att_ref.shape[1:])
        delta = jnp.sum(
            do.astype(jnp.float32) * att.astype(jnp.float32), axis=1, keepdims=True
        )
        upstream = dot(do, v, across)
        slopes = (weight.astype(jnp.float32) * (upstream - delta)).astype(jnp.bfloat16)
        dq = jnp.dot(slopes, k, preferred_element_type=jnp.float32) * scale
        dq = dq.astype(jnp.bfloat16)
        pieces = head_size // unit
        for piece in range(pieces):
            slopes_own[head * pieces + piece] = dq[:, piece * unit : (piece + 1) * unit]
        dk = dot(slopes, q, down) * scale
        terms[head, 0] = dk.astype(jnp.bfloat16).reshape(terms.shape[2:])
        dv = dot(weight, do, down)
        terms[head, 1] = dv.astype(jnp.bfloat16).reshape(terms.shape[2:])
        return carry

    def pass_on(group):
        arrived(0, group)
        start(1, group)

    def fold_sides(group):
        heads = pl.ds(group * per_group, per_group)
        arrived(2, group)
        terms[heads, :, :, 1] = terms[heads, :, :, 1] + from_side[0, heads]
        terms[heads, :, :, columns] = terms[heads, :, :, columns] + from_side[1, heads]
        start(3, group)

    def fold_rows(group):
        heads = pl.ds(group * per_group, per_group)
        arrived(3, group)
        for row in range(rows):
            value = terms[heads, :, row + 1, pl.ds(1, columns)]
            if row == 0:
                value = value + from_row[0, heads]
            if row == rows - 1:
                value = value + from_row[1, heads]
            grad_ref[heads, :, row] = value

    pass_on(0)
    if groups > 1:
        pass_on(1)
    for group in range(groups):
        arrived(1, group)
        lax.fori_loop(group * per_group, (group + 1) * per_group, head_step, 0)
        start(2, group)
        for peer in range(ha_count):
            last = ((peer + 1) * share * unit - 1) // head_size
            if last // per_group == group:

                @pl.when(peer != ha)
                def _(peer=peer):
                    slope_copy(peer).start()

                @pl.when(peer == ha)
                def _(peer=peer):
                    slopes_all[peer] = slopes_own[pl.ds(peer * share, share)]

        if group + 2 < groups:
            pass_on(group + 2)

    landed(x_all, x_recv, partner)
    for pair in range(pairs):

        @pl.when(pair != high)
        def _(pair=pair):
            forward_copy(0, partner, 2 * pair + low, pair).start()

    for pair in range(pairs):

        @pl.when(pair != high)
        def _(pair=pair):
            landed(x_all, x_recv, 2 * pair + low)
            forward_copy(1, 2 * pair + low, partner, pair).start()

    for group in range(groups):
        fold_sides(group)

    own_x.wait()
    for peer in range(ha_count):

        @pl.when(peer != ha)
        def _(peer=peer):
            landed(slopes_all, slope_recv, peer)

    for pair in range(pairs):

        @pl.when(pair != high)
        def _(pair=pair):
            slot = 2 * pair + 1 - low
            for part in range(2):
                forward_copy(part, slot, partner, pair).wait_recv()

    block = x_all.shape[2] // chips

    for step in range(chips):
        total = jnp.zeros((block, share * unit), jnp.float32)
        for peer in range(ha_count):
            left = x_all[peer, :, step * block : (step + 1) * block]
            right = jnp.concatenate([slopes_all[peer, at] for at in range(share)], axis=1)
            total = total + lax.dot_general(
                left, right, (((0,), (0,)), ((), ())), preferred_element_type=jnp.float32
            )
        product[step] = total.astype(product.dtype).reshape(product.shape[1:])
        pair_copy(step).start()

    for peer in range(chips):
        pair_copy(peer).wait_recv()
        both = product[peer, core].astype(jnp.float32) + from_partner[peer].astype(jnp.float32)
        pair_sums[peer] = both.astype(pair_sums.dtype)

        @pl.when(peer != chip)
        def _(peer=peer):
            chip_copy(peer).start()

        @pl.when(peer == chip)
        def _(peer=peer):
            from_chips[peer] = pair_sums[peer]

    for group in range(groups):
        fold_rows(group)
    for peer in range(chips):

        @pl.when(peer != chip)
        def _(peer=peer):
            landed(from_chips, chip_recv, peer)

    gathered = from_chips[0].astype(jnp.float32)
    for peer in range(1, chips):
        gathered = gathered + from_chips[peer].astype(jnp.float32)
    tokens_all = queries * ha_count * wa_count
    weight_ref[...] = (gathered * (1.0 / math.sqrt(tokens_all))).astype(weight_ref.dtype)

    for phase in range(4):
        for group in range(groups):
            sent(phase, group)
    for peer in range(ha_count):

        @pl.when(peer != ha)
        def _(peer=peer):
            slope_copy(peer).wait_send()

    x_copy(partner).wait_send()
    for pair in range(pairs):

        @pl.when(pair != high)
        def _(pair=pair):
            x_copy(2 * pair + low).wait_send()
            forward_copy(0, partner, 2 * pair + low, pair).wait_send()
            forward_copy(1, 2 * pair + low, partner, pair).wait_send()

    for peer in range(chips):
        pair_copy(peer).wait_send()

        @pl.when(peer != chip)
        def _(peer=peer):
            chip_copy(peer).wait_send()


def on_device(inputs, query_vectors, key_vectors, value_vectors, output_cotangent, window):
    frames, rows, columns, feature = query_vectors.shape
    head_count = window.shape[0]
    head_size = feature // head_count
    queries = frames * rows * columns
    groups = math.gcd(GROUPS, head_count)

    def by_head(x):
        return x.reshape(frames, rows, columns, head_count, head_size).transpose(3, 1, 2, 0, 4)

    q = by_head(query_vectors)
    do = by_head(output_cotangent)
    own = jnp.stack([by_head(key_vectors), by_head(value_vectors)], axis=1)
    bf = jnp.bfloat16
    flat_inputs = inputs.transpose(1, 2, 0, 3).reshape(queries, inputs.shape[3])
    ha_count, wa_count = lax.axis_size("ha"), lax.axis_size("wa")
    chips = wa_count // 2
    slice_rows = inputs.shape[3] // wa_count
    slice_columns = feature // ha_count
    unit = math.gcd(head_size, slice_columns)
    tall = (head_count, 2, rows + 2, columns + 2, frames, head_size)
    vmem = pl.BlockSpec(memory_space=pltpu.VMEM)
    att, grads, weight_gradient = pl.pallas_call(
        functools.partial(attention_kernel, groups),
        out_shape=(
            jax.ShapeDtypeStruct((head_count, rows, columns, frames, head_size), bf),
            jax.ShapeDtypeStruct((head_count, 2, rows, columns, frames, head_size), bf),
            jax.ShapeDtypeStruct((slice_rows, slice_columns), bf),
        ),
        in_specs=[pl.BlockSpec(memory_space=pl.ANY), vmem, vmem, vmem, vmem],
        out_specs=(vmem, vmem, vmem),
        scratch_shapes=[
            pltpu.SMEM(window.shape, window.dtype),
            pltpu.VMEM(tall, bf),
            pltpu.VMEM(tall, bf),
            pltpu.VMEM((2, head_count, 2, rows + 2, frames, head_size), bf),
            pltpu.VMEM((2, head_count, 2, columns, frames, head_size), bf),
            pltpu.VMEM((feature // unit, queries, unit), bf),
            pltpu.VMEM((ha_count, queries, inputs.shape[3]), bf),
            pltpu.VMEM((ha_count, slice_columns // unit, queries, unit), bf),
            pltpu.VMEM((chips, 2, slice_rows, slice_columns), bf),
            pltpu.VMEM((chips, slice_rows, slice_columns), bf),
            pltpu.VMEM((chips, slice_rows, slice_columns), bf),
            pltpu.VMEM((chips, slice_rows, slice_columns), bf),
            pltpu.SemaphoreType.DMA((3,)),
            pltpu.SemaphoreType.DMA((4, 2, groups)),
            pltpu.SemaphoreType.DMA((4, 2, groups)),
            pltpu.SemaphoreType.DMA((ha_count,)),
            pltpu.SemaphoreType.DMA((ha_count,)),
            pltpu.SemaphoreType.DMA((2, ha_count // 2)),
            pltpu.SemaphoreType.DMA((2, ha_count)),
            pltpu.SemaphoreType.DMA((ha_count,)),
            pltpu.SemaphoreType.DMA((ha_count,)),
            pltpu.SemaphoreType.DMA((chips,)),
            pltpu.SemaphoreType.DMA((chips,)),
            pltpu.SemaphoreType.DMA((chips,)),
            pltpu.SemaphoreType.DMA((chips,)),
        ],
        compiler_params=pltpu.CompilerParams(
            collective_id=0, has_side_effects=True, vmem_limit_bytes=56 * 1024 * 1024
        ),
    )(window, q, do, own, flat_inputs)

    def to_grid(x):
        return x.transpose(3, 1, 2, 0, 4).reshape(frames, rows, columns, feature)

    attention_output = to_grid(att)
    key_gradient = to_grid(grads[:, 0])
    value_gradient = to_grid(grads[:, 1])
    return (attention_output, key_gradient, value_gradient, weight_gradient)


def solution(mesh):
    cells = P(None, "ha", "wa", None)
    return jax.shard_map(
        on_device,
        mesh=mesh,
        in_specs=(cells, cells, cells, cells, cells, P()),
        out_specs=(cells, cells, cells, P("wa", "ha")),
        check_vma=False,
    )
```

profile of v0, /device:TPU:0, one launch (start us, length us, event | category | flops | bytes accessed | tf_op | source)
XLA Modules:
  0.0 75.5 jit_solution(6565562286205045608)
XLA Ops:
  0.6 1.4 %copy.21.window_hbm = s32[12,4]{1,0:T(8,128)} copy(s32[12,4]{0,1:T(4,128)} %param.11) | data formatting | bytes 384 | tf_op args[5]
  2.0 1.9 %copy.20 = bf16[2,2,32,1536]{3,2,1,0:T(8,128)(2,1)} copy(bf16[2,2,32,1536]{3,1,0,2:T(2,128)(2,1)} %bitcast.25) | data formatting | bytes 786432 | tf_op jit(solution)/shard_map/transpose | solution.py:447
  3.9 0.0 copy-done.1
  3.9 0.3 reshape.40
  4.1 0.7 copy-done.2
  4.9 0.3 reshape.42
  5.1 0.7 copy-done.3
  5.8 0.3 reshape.43
  6.1 0.5 copy_bitcast_fusion
  6.6 0.0 copy-start.4
  6.6 1.0 %pad_maximum_fusion.own_ref = bf16[12,2,2,2,32,128]{5,4,3,2,1,0:T(8,128)(2,1)} fusion(bf16[12,1,2,2,32,128]{5,4,3,2,1,0:T(8,128)(2,1)S(1)} %get-tuple-element.16, bf16[12,1,2,2,32,128]{5,4,3,2,1,0:T(8,128)(2,1)S(1)} %get-tuple-element.17), kind=kLoop, calls=%fused_computation | loop fusion | flops 393216 | bytes 1572864 | tf_op jit(solution)/shard_map/stack | solution.py:445
  7.6 0.1 copy-done.4
  7.7 0.3 reshape.41
  8.0 1.4 %copy_bitcast_fusion.2 = (bf16[12,2,2,32,128]{4,3,2,1,0:T(8,128)(2,1)}, bf16[12,2,2,32,128]{4,3,2,1,0:T(8,128)(2,1)}) fusion(bf16[32,2,2,12,128]{4,3,2,1,0:T(8,128)(2,1)S(1)} %reshape.41, bf16[32,2,2,12,128]{4,3,2,1,0:T(8,128)(2,1)S(1)} %reshape.40), kind=kLoop, calls=%fused_computation.3 | loop fusion | bytes 1572864 | tf_op jit(solution)/shard_map/transpose | solution.py:441
  9.3 60.7 %shard_map.93 = (bf16[12,2,2,32,128]{4,3,2,1,0:T(8,128)(2,1)}, bf16[12,2,2,2,32,128]{5,4,3,2,1,0:T(8,128)(2,1)}, bf16[192,384]{1,0:T(8,128)(2,1)}) custom-call(s32[12,4]{1,0:T(8,128)} %copy.21.window_hbm, bf16[12,2,2,32,128]{4,3,2,1,0:T(8,128)(2,1)} %get-tuple-element.19.q_ref, bf16[12,2,2,32,128]{4,3,2,1,0:T(8,128)(2,1)} %get-tuple-element.18.do_ref, ...), custom_call_target="tpu_custom_call" | custom-call | tf_op jit(solution)/shard_map/pallas_call | solution.py:455
  70.1 1.3 %copy.36 = bf16[32,2,2,12,128]{4,3,2,1,0:T(8,128)(2,1)S(1)} copy(bf16[32,2,2,12,128]{4,0,2,1,3:T(8,128)(2,1)} %bitcast.24) | data formatting | bytes 786432
  71.4 0.9 %reshape.44 = bf16[32,2,2,1536]{3,2,1,0:T(2,128)(2,1)} reshape(bf16[32,2,2,12,128]{4,3,2,1,0:T(8,128)(2,1)S(1)} %copy.36) | data formatting | bytes 786432
  72.3 0.0 copy-done
  72.3 0.1 slice_bitcast_fusion
  72.4 0.3 copy.38
  72.7 0.9 %reshape.46 = bf16[32,2,2,1536]{3,2,1,0:T(2,128)(2,1)} reshape(bf16[32,2,2,12,128]{4,3,2,1,0:T(8,128)(2,1)S(1)} %copy.38) | data formatting | bytes 786432
  73.6 0.3 copy.37
  73.9 0.9 %reshape.45 = bf16[32,2,2,1536]{3,2,1,0:T(2,128)(2,1)} reshape(bf16[32,2,2,12,128]{4,3,2,1,0:T(8,128)(2,1)S(1)} %copy.37) | data formatting | bytes 786432
  74.8 0.7 copy.47
  (6 shorter events, 0.0 us)
Async XLA Ops:
  2.0 1.9 %copy-start.1 = (bf16[32,2,2,1536]{3,2,1,0:T(2,128)(2,1)S(1)}, bf16[32,2,2,1536]{3,2,1,0:T(2,128)(2,1)}, u32[]{:S(2)}) copy-start(bf16[32,2,2,1536]{3,2,1,0:T(2,128)(2,1)} %param.7) | copy-start | bytes 1179652
  3.9 1.0 %copy-start.2 = (bf16[32,2,2,1536]{3,2,1,0:T(2,128)(2,1)S(1)}, bf16[32,2,2,1536]{3,2,1,0:T(2,128)(2,1)}, u32[]{:S(2)}) copy-start(bf16[32,2,2,1536]{3,2,1,0:T(2,128)(2,1)} %param.8) | copy-start | bytes 1179652
  4.9 1.0 %copy-start.3 = (bf16[32,2,2,1536]{3,2,1,0:T(2,128)(2,1)S(1)}, bf16[32,2,2,1536]{3,2,1,0:T(2,128)(2,1)}, u32[]{:S(2)}) copy-start(bf16[32,2,2,1536]{3,2,1,0:T(2,128)(2,1)} %param.9) | copy-start | bytes 1179652
  6.6 1.0 %copy-start.4 = (bf16[32,2,2,1536]{3,2,1,0:T(2,128)(2,1)S(1)}, bf16[32,2,2,1536]{3,2,1,0:T(2,128)(2,1)}, u32[]{:S(2)}) copy-start(bf16[32,2,2,1536]{3,2,1,0:T(2,128)(2,1)} %param.10) | copy-start | bytes 1179652
  70.1 2.3 %copy-start = (bf16[12,2,2,2,32,128]{5,4,3,2,1,0:T(8,128)(2,1)S(1)}, bf16[12,2,2,2,32,128]{5,4,3,2,1,0:T(8,128)(2,1)}, u32[]{:S(2)}) copy-start(bf16[12,2,2,2,32,128]{5,4,3,2,1,0:T(8,128)(2,1)} %get-tuple-element.8) | copy-start | bytes 2359300
  73.9 0.9 %copy-start.5 = (bf16[192,384]{1,0:T(8,128)(2,1)S(1)}, bf16[192,384]{1,0:T(8,128)(2,1)}, u32[]{:S(2)}) copy-start(bf16[192,384]{1,0:T(8,128)(2,1)} %get-tuple-element.27) | copy-start | bytes 442372
where the time goes:
time: 76 us; the launch traced here: 75.5 us
  Pallas kernels  60.7 us (80%)
  local copies, waits for them, and re-layouts  13.1 us (17%)
  other arithmetic  0.95 us (1%)
    pallas_call x1, Pallas kernels, on_device(): pl.pallas_call(functools.partial(attention_kernel, groups), out_shape=(ja...  60.7 us
    unnamed x20, local copies, waits for them, and re-layouts  8.22 us
    transpose x1, local copies, waits for them, and re-layouts, on_device(): flat_inputs = inputs.transpose(1, 2, 0, 3).reshape(queries, inputs.shape[3])  1.86 us

commit v1 on v0

--- a/solution.py
+++ b/solution.py
@@ -430,7 +430,7 @@
             chip_copy(peer).wait_send()
 
 
-def on_device(inputs, query_vectors, key_vectors, value_vectors, output_cotangent, window):
+def on_device(branch, inputs, query_vectors, key_vectors, value_vectors, output_cotangent, window):
     frames, rows, columns, feature = query_vectors.shape
     head_count = window.shape[0]
     head_size = feature // head_count
@@ -489,7 +489,7 @@
             pltpu.SemaphoreType.DMA((chips,)),
         ],
         compiler_params=pltpu.CompilerParams(
-            collective_id=0, has_side_effects=True, vmem_limit_bytes=56 * 1024 * 1024
+            collective_id=branch, has_side_effects=True, vmem_limit_bytes=56 * 1024 * 1024
         ),
     )(window, q, do, own, flat_inputs)
 
@@ -502,10 +502,15 @@
     return (attention_output, key_gradient, value_gradient, weight_gradient)
 
 
+def by_reach(*args):
+    many = jnp.sum(args[5][:, 2]) > 6
+    return lax.cond(many, functools.partial(on_device, 1), functools.partial(on_device, 0), *args)
+
+
 def solution(mesh):
     cells = P(None, "ha", "wa", None)
     return jax.shard_map(
-        on_device,
+        by_reach,
         mesh=mesh,
         in_specs=(cells, cells, cells, cells, cells, P()),
         out_specs=(cells, cells, cells, P("wa", "ha")),

time: 76 us -> 75.7 us (level)
  local copies, waits for them, and re-layouts: 13.1 us -> 10.6 us
  other arithmetic: 0.95 us -> 2.28 us
    unnamed x20 -> x9, local copies, waits for them, and re-layouts: 8.22 us -> 1.04 us
    cond x0 -> x16, local copies, waits for them, and re-layouts: none -> 3.95 us
    another operation x0 -> x2, local copies, waits for them, and re-layouts: none -> 2.54 us
    transpose x1 -> x0, local copies, waits for them, and re-layouts: 1.86 us -> none  [on_device(): flat_inputs = inputs.transpose(1, 2, 0, 3).reshape(queries, inputs.shape[3])]
    reduce_sum x0 -> x1, other arithmetic: none -> 1.32 us  [by_reach(): many = jnp.sum(args[5][:, 2]) > 6]
where the time goes in v1:
time: 75.7 us; the launch traced here: 75.3 us
  Pallas kernels  60.7 us (80%)
  local copies, waits for them, and re-layouts  10.6 us (14%)
  other arithmetic  2.28 us (3%)
  between operations  1.33 us (2%)
    pallas_call x1, Pallas kernels, on_device(): pl.pallas_call(functools.partial(attention_kernel, groups), out_shape=(ja...  60.7 us
    cond x16, local copies, waits for them, and re-layouts  3.95 us
    another operation x2, local copies, waits for them, and re-layouts  2.54 us

profile of v1, /device:TPU:0, one launch (start us, length us, event | category | flops | bytes accessed | tf_op | source)
XLA Modules:
  0.0 75.3 jit_solution(7937378794616506912)
XLA Ops:
  0.6 1.3 %slice_reduce_fusion = s32[]{:T(128)} fusion(s32[12,4]{0,1:T(4,128)} %param.13), kind=kLoop, calls=%fused_computation.14 | loop fusion | flops 11 | bytes 52 | tf_op jit(solution)/shard_map/reduce_sum | solution.py:506
  2.6 71.6 %conditional.1 = (bf16[192,384]{1,0:T(8,128)(2,1)S(1)}, bf16[32,2,2,1536]{3,2,1,0:T(2,128)(2,1)S(1)}, bf16[32,2,2,1536]{3,2,1,0:T(2,128)(2,1)S(1)}, bf16[32,2,2,1536]{3,2,1,0:T(2,128)(2,1)S(1)}) conditional(s32[]{:T(128)} %convert_element_type.3, (bf16[32,2,2,1536]{3,2,1,0:T(2,128)(2,1)}, bf16[32,2,2,1536]{3,2,1,0:T(2,128)(2,1)}, ...), branch_computations={%region_1.0_spmd, %region_2.0_spmd} | conditional | flops 393216 | bytes 24379948 | solution.py:507
  2.8 0.7 copy.45.window_hbm
  3.5 1.9 %copy.44 = bf16[32,2,2,1536]{3,0,2,1:T(8,128)(2,1)} copy(bf16[32,2,2,1536]{3,2,1,0:T(2,128)(2,1)} %get-tuple-element.71) | data formatting | bytes 786432 | tf_op jit(solution)/shard_map
  5.4 0.3 reshape.66
  5.7 0.7 copy-done.5
  6.4 0.3 reshape.65
  6.6 0.5 copy_bitcast_fusion.4
  7.2 1.0 %pad_maximum_fusion.1.own_ref = bf16[12,2,2,2,32,128]{5,4,3,2,1,0:T(8,128)(2,1)} fusion(bf16[12,1,2,2,32,128]{5,4,3,2,1,0:T(8,128)(2,1)S(1)} %get-tuple-element.88, bf16[12,1,2,2,32,128]{5,4,3,2,1,0:T(8,128)(2,1)S(1)} %get-tuple-element.89), kind=kLoop, calls=%fused_computation.7 | loop fusion | flops 393216 | bytes 1572864 | tf_op jit(solution)/shard_map/cond/branch_1_fun/stack | solution.py:445
  8.1 0.1 copy-done.3
  8.2 0.3 reshape.64
  8.5 0.7 copy-done.1
  9.2 0.3 reshape.63
  9.5 1.4 %copy_bitcast_fusion.6 = (bf16[12,2,2,32,128]{4,3,2,1,0:T(8,128)(2,1)}, bf16[12,2,2,32,128]{4,3,2,1,0:T(8,128)(2,1)}) fusion(bf16[32,2,2,12,128]{4,3,2,1,0:T(8,128)(2,1)S(1)} %reshape.64, bf16[32,2,2,12,128]{4,3,2,1,0:T(8,128)(2,1)S(1)} %reshape.63), kind=kLoop, calls=%fused_computation.10 | loop fusion | bytes 1572864 | tf_op jit(solution)/shard_map/cond/branch_1_fun/transpose | solution.py:441
  10.9 60.7 %branch_1_fun.1 = (bf16[12,2,2,32,128]{4,3,2,1,0:T(8,128)(2,1)}, bf16[12,2,2,2,32,128]{5,4,3,2,1,0:T(8,128)(2,1)}, bf16[192,384]{1,0:T(8,128)(2,1)S(1)}) custom-call(s32[12,4]{1,0:T(8,128)} %copy.45.window_hbm, bf16[12,2,2,32,128]{4,3,2,1,0:T(8,128)(2,1)} %get-tuple-element.91.q_ref, bf16[12,2,2,32,128]{4,3,2,1,0:T(8,128)(2,1)} %get-tuple-element.90.do_ref, ...), custom_call_target="tpu_custom_call" | custom-call | tf_op jit(solution)/shard_map/cond/branch_1_fun/pallas_call | solution.py:455
  71.5 1.3 %copy.77 = bf16[32,2,2,12,128]{4,3,2,1,0:T(8,128)(2,1)S(1)} copy(bf16[32,2,2,12,128]{4,0,2,1,3:T(8,128)(2,1)} %bitcast.51) | data formatting | bytes 786432 | tf_op jit(solution)/shard_map/cond
  72.9 0.2 reshape.67
  73.1 0.3 copy.79
  73.4 0.2 reshape.69
  73.6 0.3 copy.78
  73.9 0.2 reshape.68
  74.3 0.8 copy.100
  75.1 0.1 copy-done.11
  75.2 0.1 copy-done.12
  (14 shorter events, 0.1 us)
Async XLA Ops:
  2.0 0.7 copy-start.13
  3.5 1.9 %copy-start.7 = (bf16[32,2,2,1536]{3,2,1,0:T(2,128)(2,1)S(1)}, bf16[32,2,2,1536]{3,2,1,0:T(2,128)(2,1)}, u32[]{:S(2)}) copy-start(bf16[32,2,2,1536]{3,2,1,0:T(2,128)(2,1)} %get-tuple-element.70) | copy-start | bytes 1179652 | tf_op jit(solution)/shard_map/cond
  5.4 1.0 %copy-start.5 = (bf16[32,2,2,1536]{3,2,1,0:T(2,128)(2,1)S(1)}, bf16[32,2,2,1536]{3,2,1,0:T(2,128)(2,1)}, u32[]{:S(2)}) copy-start(bf16[32,2,2,1536]{3,2,1,0:T(2,128)(2,1)} %get-tuple-element.69) | copy-start | bytes 1179652 | tf_op jit(solution)/shard_map/cond
  7.2 1.0 %copy-start.3 = (bf16[32,2,2,1536]{3,2,1,0:T(2,128)(2,1)S(1)}, bf16[32,2,2,1536]{3,2,1,0:T(2,128)(2,1)}, u32[]{:S(2)}) copy-start(bf16[32,2,2,1536]{3,2,1,0:T(2,128)(2,1)} %get-tuple-element.68) | copy-start | bytes 1179652 | tf_op jit(solution)/shard_map/cond
  8.2 1.0 %copy-start.1 = (bf16[32,2,2,1536]{3,2,1,0:T(2,128)(2,1)S(1)}, bf16[32,2,2,1536]{3,2,1,0:T(2,128)(2,1)}, u32[]{:S(2)}) copy-start(bf16[32,2,2,1536]{3,2,1,0:T(2,128)(2,1)} %get-tuple-element.67) | copy-start | bytes 1179652 | tf_op jit(solution)/shard_map/cond
  71.5 1.5 %copy-start.9 = (bf16[12,2,2,2,32,128]{5,4,3,2,1,0:T(8,128)(2,1)S(1)}, bf16[12,2,2,2,32,128]{5,4,3,2,1,0:T(8,128)(2,1)}, u32[]{:S(2)}) copy-start(bf16[12,2,2,2,32,128]{5,4,3,2,1,0:T(8,128)(2,1)} %get-tuple-element.40) | copy-start | bytes 2359300 | tf_op jit(solution)/shard_map/cond
  74.3 0.8 %copy-start.10 = (bf16[32,2,2,1536]{3,2,1,0:T(2,128)(2,1)}, bf16[32,2,2,1536]{3,2,1,0:T(2,128)(2,1)S(1)}, u32[]{:S(2)}) copy-start(bf16[32,2,2,1536]{3,2,1,0:T(2,128)(2,1)S(1)} %get-tuple-element.104) | copy-start | bytes 1179652
  74.3 0.9 %copy-start.11 = (bf16[32,2,2,1536]{3,2,1,0:T(2,128)(2,1)}, bf16[32,2,2,1536]{3,2,1,0:T(2,128)(2,1)S(1)}, u32[]{:S(2)}) copy-start(bf16[32,2,2,1536]{3,2,1,0:T(2,128)(2,1)S(1)} %get-tuple-element.106) | copy-start | bytes 1179652
  74.3 1.0 %copy-start.12 = (bf16[32,2,2,1536]{3,2,1,0:T(2,128)(2,1)}, bf16[32,2,2,1536]{3,2,1,0:T(2,128)(2,1)S(1)}, u32[]{:S(2)}) copy-start(bf16[32,2,2,1536]{3,2,1,0:T(2,128)(2,1)S(1)} %get-tuple-element.105) | copy-start | bytes 1179652
